TPU v7x, 128 devices: a whole 4x4x4 slice. The times are simulated.
128 devices in a mesh: chan: 32 (over z_lo, y, x), seg: 4 (over z_hi, core).
Axes of the slice: x: 4, y: 4, z: 4 (z_hi: 2, z_lo: 2; z = z_hi * 2 + z_lo), core: 2. Of those that a mesh axis runs over, the one named last changes fastest.
Arguments:
- traces: bfloat16 [4096, 8, 8192], P('chan', 'seg'), may hold values from -20 to 20
- pair_offsets: int32 [32, 16], replicated, may hold values from 1 to 31, as said below
- pair_counts: int32 [32], replicated, may hold values from 1 to 16, 64 in all
- pair_owner: int32 [64], replicated, may hold values from 0 to 63, each once
Outputs:
- correlations: float32 [128, 64, 128, 256], P('seg', 'chan')
Inputs may be any that keep to these rules, and one draw needn't show every extreme that they name: `pair_offsets`: row a lists 16 distinct offsets; only its first pair_counts[a] entries name pairs. `pair_counts`: the counts sum to 64. `pair_owner`: every slot number appears once.
All inputs are finite; a program needn't handle non-finite values.
Results may differ from a plain program's by a relative error of at most 0.017.
Values may be sent and summed in bfloat16 or wider, within the bound.
No kernel may reach another device: no remote copies, remote signals or barrier semaphores. Data moves between devices by JAX's collectives and lax.ppermute only.
A program may use at most 128 MiB of HBM per device.

v0:
```python
import math
import jax
import jax.numpy as jnp
from jax import lax
from jax.sharding import PartitionSpec as P

SAMPLES = 8192
BAND_START = 32
FREQS = 512
HALF = 8
LAGS = 256
TILE_DEV = 2


def smoother(bin_count):
    bins_axis = lax.iota(jnp.int32, bin_count)
    nearby = (jnp.abs(bins_axis[:, None] - bins_axis[None, :]) <= HALF).astype(jnp.float32)
    return nearby / jnp.sum(nearby, axis=0, keepdims=True)


def lag_table(first_bin, bin_count):
    bins_axis = BAND_START + first_bin + lax.iota(jnp.int32, bin_count)
    shifts = jnp.mod(lax.iota(jnp.int32, LAGS) - LAGS // 2, SAMPLES)
    phase_index = jnp.mod(bins_axis[:, None] * shifts[None, :], SAMPLES)
    angles = phase_index.astype(jnp.float32) * (2.0 * math.pi / SAMPLES)
    return jnp.concatenate([jnp.cos(angles), -jnp.sin(angles)], axis=0).astype(jnp.bfloat16)


def pair_blocks(pair_offsets, pair_counts, pair_owner, block_count, slot_count):
    slot_index = lax.iota(jnp.int32, slot_count)
    starts = jnp.cumsum(pair_counts) - pair_counts
    first_block = jnp.sum((starts[None, :] <= slot_index[:, None]).astype(jnp.int32), axis=1) - 1
    member = lax.iota(jnp.int32, block_count)[None, :] == first_block[:, None]
    start_of = jnp.sum(jnp.where(member, starts[None, :], 0), axis=1)
    position = slot_index - start_of
    listed = jnp.sum(jnp.where(member[:, :, None], pair_offsets[None, :, :], 0), axis=1)
    chosen = lax.iota(jnp.int32, pair_offsets.shape[1])[None, :] == position[:, None]
    offset = jnp.sum(jnp.where(chosen, listed, 0), axis=1)
    second_block = jnp.mod(first_block + offset, block_count)
    held = pair_owner[None, :] == slot_index[:, None]
    slot_first = jnp.sum(jnp.where(held, first_block[None, :], 0), axis=1)
    slot_second = jnp.sum(jnp.where(held, second_block[None, :], 0), axis=1)
    return (slot_first, slot_second)


def cross_terms(first_spec, second_spec):
    turned = jnp.stack([first_spec[:, :, :, 1], -first_spec[:, :, :, 0]], axis=3)
    real_part = jnp.einsum(
        "tispf,tjspf->itjf", first_spec, second_spec, preferred_element_type=jnp.float32
    )
    imag_part = jnp.einsum(
        "tispf,tjspf->itjf", turned, second_spec, preferred_element_type=jnp.float32
    )
    return jnp.stack([real_part, imag_part], axis=3).astype(jnp.bfloat16)


def invert(spectra, table, norm_factor):
    flat = spectra.reshape(-1, spectra.shape[3] * spectra.shape[4])
    lagged = jnp.dot(flat, table, preferred_element_type=jnp.float32) * norm_factor
    return lagged.reshape(spectra.shape[:3] + (table.shape[1],))


def on_device(traces, pair_offsets, pair_counts, pair_owner):
    block_size, local_segs, sample_count = traces.shape
    parts_count = lax.axis_size("seg")
    block_count = lax.axis_size("chan")
    quarter_bins = FREQS // parts_count
    all_segs = local_segs * parts_count
    norm_factor = 1.0 / math.sqrt(FREQS * all_segs)
    signal = traces.reshape(block_size * local_segs, sample_count)
    width_bins = min(128, FREQS)
    pieces_count = FREQS // width_bins
    times_axis = lax.iota(jnp.int32, sample_count)

    def transform(piece_index):
        bins_axis = BAND_START + piece_index * width_bins + lax.iota(jnp.int32, width_bins)
        phase_index = jnp.mod(times_axis[:, None] * bins_axis[None, :], sample_count)
        angles = phase_index.astype(jnp.float32) * (2.0 * math.pi / sample_count)
        table_part = jnp.concatenate([jnp.cos(angles), -jnp.sin(angles)], axis=1)
        table_high = table_part.astype(jnp.bfloat16)
        table_low = (table_part - table_high.astype(jnp.float32)).astype(jnp.bfloat16)
        upper = jnp.dot(signal, table_high, preferred_element_type=jnp.float32)
        return upper + jnp.dot(signal, table_low, preferred_element_type=jnp.float32)

    spectrum = lax.map(transform, lax.iota(jnp.int32, pieces_count))
    spectrum = (
        spectrum.reshape(pieces_count, -1, 2, width_bins)
        .transpose(1, 2, 0, 3)
        .reshape(-1, 2, FREQS)
    )
    real_part = spectrum[:, 0]
    imag_part = spectrum[:, 1]
    amplitude = jnp.sqrt(real_part * real_part + imag_part * imag_part)
    smoothed = jnp.dot(
        amplitude,
        smoother(FREQS),
        precision=lax.Precision.HIGHEST,
        preferred_element_type=jnp.float32,
    )
    divisor = jnp.maximum(smoothed, 1.0)
    whitened = jnp.stack([real_part / divisor, imag_part / divisor], axis=1).astype(jnp.bfloat16)
    whitened = whitened.reshape(block_size, local_segs, 2, parts_count, quarter_bins)
    quarter = lax.all_to_all(whitened, "seg", split_axis=3, concat_axis=1, tiled=True)
    quarter = quarter.reshape(block_size, all_segs, 2, quarter_bins)
    slot_first, slot_second = pair_blocks(
        pair_offsets, pair_counts, pair_owner, block_count, TILE_DEV * block_count
    )
    my_start = lax.axis_index("chan") * TILE_DEV
    needed = jnp.concatenate(
        [
            lax.dynamic_slice_in_dim(slot_first, my_start, TILE_DEV),
            lax.dynamic_slice_in_dim(slot_second, my_start, TILE_DEV),
        ]
    )
    empty_blocks = jnp.zeros((2 * TILE_DEV, block_size, all_segs, 2, quarter_bins), jnp.bfloat16)
    incoming = lax.all_gather(quarter, "chan", axis=0, tiled=True)
    block_total = incoming.shape[0] // block_size
    incoming_blocks = incoming.reshape(block_total, block_size, all_segs, 2, quarter_bins)
    inside = (needed >= 0) & (needed < block_total)
    picked = jnp.take(incoming_blocks, jnp.clip(needed, 0, block_total - 1), axis=0)
    held_blocks = jnp.where(inside[:, None, None, None, None], picked, empty_blocks)
    first_spec = held_blocks[:TILE_DEV]
    second_spec = held_blocks[TILE_DEV:]
    full_table = lag_table(0, FREQS)
    spectra = cross_terms(first_spec, second_spec)
    return invert(
        lax.all_to_all(spectra, "seg", split_axis=0, concat_axis=4, tiled=True),
        full_table,
        norm_factor,
    )


def solution(mesh):
    placed = (P("chan", "seg", None), P(), P(), P())
    return jax.shard_map(
        on_device,
        mesh=mesh,
        in_specs=placed,
        out_specs=P("seg", "chan", None, None),
        check_vma=False,
    )
```

profile of v0, /device:TPU:1, one launch (start us, length us, event | category | flops | bytes accessed | tf_op | source)
XLA Modules:
  0.0 643.9 jit_solution(6079321119400441198)
XLA Ops:
  6.5 0.1 convert_reduce_fusion
  6.6 7.2 %reshape.215 = bf16[256,8192]{1,0:T(8,128)(2,1)} reshape(bf16[128,2,8192]{2,1,0:T(2,128)(2,1)} %param.6) | data formatting | bytes 8388608 | tf_op jit(solution)/shard_map/reshape | solution.py:70
  13.8 82.4 %while.13 = (s32[]{:T(128)}, f32[4,256,256]{1,2,0:T(8,128)S(1)}, s32[4]{0:T(128)S(1)}, bf16[256,8192]{1,0:T(8,128)(2,1)}, s32[]{:T(128)}, /*index=5*/s32[1]{0:T(128)}, s32[1]{0:T(128)}) while((s32[]{:T(128)}, f32[4,256,256]{1,2,0:T(8,128)S(1)}, s32[4]{0:T(128)S(1)}, bf16[256,8192]{1,0:T(8,128)(2,1)}, s32[]{:T(128)}, ...), condition=%wide.region_8.9_spmd.clone, body=%wide.region_7.8_spmd.clone.sunk | while | flops 2182152192 | bytes 51119252 | solution.py:85
  13.8 0.7 dynamic_slice.19
  15.2 16.5 %fusion.57 = (f32[8192,128]{1,0:T(8,128)S(1)}, f32[8192,128]{1,0:T(8,128)S(1)}) fusion(s32[128]{0:T(128)S(1)} %iota_add_fusion.3), kind=kLoop, calls=%fused_computation.18.clone.1 | loop fusion | flops 15728640 | bytes 8389120 | tf_op jit(solution)/shard_map/while/body/eval_jaxpr/cos | solution.py:79
  31.7 1.3 fusion.58
  33.0 1.3 fusion.59
  34.4 0.7 dynamic_slice.19
  35.7 16.5 %fusion.57 = (f32[8192,128]{1,0:T(8,128)S(1)}, f32[8192,128]{1,0:T(8,128)S(1)}) fusion(s32[128]{0:T(128)S(1)} %iota_add_fusion.3), kind=kLoop, calls=%fused_computation.18.clone.1 | loop fusion | flops 15728640 | bytes 8389120 | tf_op jit(solution)/shard_map/while/body/eval_jaxpr/cos | solution.py:79
  52.3 1.3 fusion.58
  53.6 1.3 fusion.59
  54.9 0.7 dynamic_slice.19
  56.3 16.5 %fusion.57 = (f32[8192,128]{1,0:T(8,128)S(1)}, f32[8192,128]{1,0:T(8,128)S(1)}) fusion(s32[128]{0:T(128)S(1)} %iota_add_fusion.3), kind=kLoop, calls=%fused_computation.18.clone.1 | loop fusion | flops 15728640 | bytes 8389120 | tf_op jit(solution)/shard_map/while/body/eval_jaxpr/cos | solution.py:79
  72.8 1.3 fusion.58
  74.1 1.3 fusion.59
  75.5 0.7 dynamic_slice.19
  76.9 16.5 %fusion.57 = (f32[8192,128]{1,0:T(8,128)S(1)}, f32[8192,128]{1,0:T(8,128)S(1)}) fusion(s32[128]{0:T(128)S(1)} %iota_add_fusion.3), kind=kLoop, calls=%fused_computation.18.clone.1 | loop fusion | flops 15728640 | bytes 8389120 | tf_op jit(solution)/shard_map/while/body/eval_jaxpr/cos | solution.py:79
  93.4 1.3 fusion.58
  94.7 1.3 fusion.59
  96.2 0.4 copy.29
  96.6 0.4 reshape.217
  97.0 1.2 divide_convert_fusion.1
  98.6 15.9 %all_to_all.30 = bf16[128,2,2,4,128]{4,0,2,1,3:T(8,128)(2,1)} all-to-all(bf16[128,2,2,4,128]{4,0,2,1,3:T(8,128)(2,1)S(1)} %pad_maximum_fusion.2), channel_id=1, replica_groups=mesh['chan'=32,'seg'=4] {'seg'}, dimensions={3} | all-to-all | bytes 1048576 | tf_op jit(solution)/shard_map/all_to_all | solution.py:103
  114.5 0.1 copy.27
  114.6 0.1 reduce
  114.8 0.1 convert_reduce_fusion.1
  114.9 0.1 select_reduce_fusion.3
  115.0 0.1 select_reduce_fusion
  115.2 0.1 select_reduce_fusion.2
  115.3 0.1 dynamic_slice.13
  115.6 0.1 fusion.38
  115.7 0.1 compare_and_fusion.1
  115.8 186.4 %all-gather.2.cloned.1.call-done = bf16[4096,8,2,128]{3,0,2,1:T(8,128)(2,1)} async-done(((bf16[128,8,2,128]{3,0,2,1:T(8,128)(2,1)}), bf16[4096,8,2,128]{3,0,2,1:T(8,128)(2,1)}) %all-gather.2.cloned.1.call-update) | async-done | bytes 16777232 | tf_op jit(solution)/shard_map/all_gather | solution.py:116
  302.2 18.6 %copy.32 = bf16[4096,8,2,128]{3,1,2,0:T(8,128)(2,1)} copy(bf16[4096,8,2,128]{3,0,2,1:T(8,128)(2,1)} %all-gather.2.cloned.1.call-done) | data formatting | bytes 33554432 | tf_op jit(solution)/shard_map/all_gather | solution.py:116
  320.7 7.9 %gather_fusion = bf16[4,128,8,2,128]{4,2,3,1,0:T(8,128)(2,1)} fusion(bf16[32,128,8,2,128]{4,2,3,1,0:T(8,128)(2,1)} %bitcast.77, s32[1024]{0:T(1024)S(1)} %pad_clamp_fusion), kind=kCustom, calls=%fused_computation | custom fusion | bytes 4194320 | tf_op jit(solution)/shard_map/jit(_take)/gather | solution.py:120
  328.6 4.2 copy.33
  332.9 0.3 select_select_fusion
  333.2 0.1 fusion.42
  333.3 4.9 fusion.18
  338.2 4.9 fusion.19
  343.1 6.8 %pad_maximum_fusion.1 = bf16[128,2,128,2,128]{0,2,4,1,3:T(8,128)(2,1)} fusion(bf16[128,2,128,1,128]{0,2,4,1,3:T(8,128)(2,1)S(1)} %fusion.19, bf16[128,2,128,1,128]{0,2,4,1,3:T(8,128)(2,1)S(1)} %fusion.18), kind=kLoop, calls=%fused_computation.25 | loop fusion | flops 8388608 | bytes 33554432 | tf_op jit(solution)/shard_map/stack | solution.py:54
  349.9 23.5 %copy.34 = bf16[128,2,128,2,128]{2,4,1,3,0:T(8,128)(2,1)} copy(bf16[128,2,128,2,128]{0,2,4,1,3:T(8,128)(2,1)} %pad_maximum_fusion.1) | data formatting | bytes 33554432 | tf_op jit(solution)/shard_map/stack | solution.py:54
  373.4 12.9 %all-to-all-start.1 = ((bf16[128,2,128,2,128]{2,4,1,3,0:T(8,128)(2,1)}), bf16[128,2,128,2,128]{2,4,1,3,0:T(8,128)(2,1)}, u32[]{:S(2)}, u32[]{:S(2)}) async-start(bf16[128,2,128,2,128]{2,4,1,3,0:T(8,128)(2,1)} %copy.34), calls=%async_computation.1 | async-start | bytes 33554432 | tf_op jit(solution)/shard_map/all_to_all | solution.py:127
  386.3 2.5 cosine_convert_fusion
  388.8 181.2 %all-to-all-done.1 = bf16[128,2,128,2,128]{2,4,1,3,0:T(8,128)(2,1)} async-done(((bf16[128,2,128,2,128]{2,4,1,3,0:T(8,128)(2,1)}), bf16[128,2,128,2,128]{2,4,1,3,0:T(8,128)(2,1)}, u32[]{:S(2)}, u32[]{:S(2)}) %all-to-all-start.1) | async-done | bytes 16777248 | tf_op jit(solution)/shard_map/all_to_all | solution.py:127
  570.0 26.0 %copy.36 = bf16[32,2,128,2,4,128]{5,4,3,2,1,0:T(4,128)(2,1)} copy(bf16[32,2,128,2,4,128]{2,5,1,3,0,4:T(8,128)(2,1)} %bitcast.22) | data formatting | bytes 33554432 | tf_op jit(solution)/shard_map/all_to_all | solution.py:127
  596.0 27.3 %reshape.220 = bf16[8192,1024]{1,0:T(8,128)(2,1)} reshape(bf16[32,2,128,2,4,128]{5,4,3,2,1,0:T(4,128)(2,1)} %copy.36) | data formatting | bytes 33554432 | tf_op jit(solution)/shard_map/reshape | solution.py:58
  623.4 13.7 %convolution_multiply_fusion = f32[8192,256]{1,0:T(8,128)} fusion(bf16[8192,1024]{1,0:T(8,128)(2,1)} %reshape.220, bf16[512,256]{1,0:T(8,128)(2,1)S(1)} %get-tuple-element.99, bf16[512,256]{1,0:T(8,128)(2,1)S(1)} %get-tuple-element.98), kind=kOutput, calls=%fused_computation.28 | convolution fusion | flops 4298113024 | bytes 25690112 | tf_op jit(solution)/shard_map/dot_general | solution.py:59
  (41 shorter events, 0.8 us)
Async XLA Ops:
  6.5 295.6 %all-gather.2.cloned.1.call-start = ((), (), s32[]{:S(2)}) async-start(), calls=%async_computation.2 | async-start | bytes 17301504 | tf_op jit(solution)/shard_map/all_gather | solution.py:116
  15.2 16.5 %copy-start = (bf16[256,8192]{1,0:T(8,128)(2,1)S(1)}, bf16[256,8192]{1,0:T(8,128)(2,1)}, u32[]{:S(2)}) copy-start(bf16[256,8192]{1,0:T(8,128)(2,1)} %get-tuple-element.148) | copy-start | bytes 12582916 | tf_op jit(solution)/shard_map/while
  35.7 16.5 %copy-start = (bf16[256,8192]{1,0:T(8,128)(2,1)S(1)}, bf16[256,8192]{1,0:T(8,128)(2,1)}, u32[]{:S(2)}) copy-start(bf16[256,8192]{1,0:T(8,128)(2,1)} %get-tuple-element.148) | copy-start | bytes 12582916 | tf_op jit(solution)/shard_map/while
  56.3 16.5 %copy-start = (bf16[256,8192]{1,0:T(8,128)(2,1)S(1)}, bf16[256,8192]{1,0:T(8,128)(2,1)}, u32[]{:S(2)}) copy-start(bf16[256,8192]{1,0:T(8,128)(2,1)} %get-tuple-element.148) | copy-start | bytes 12582916 | tf_op jit(solution)/shard_map/while
  76.8 16.5 %copy-start = (bf16[256,8192]{1,0:T(8,128)(2,1)S(1)}, bf16[256,8192]{1,0:T(8,128)(2,1)}, u32[]{:S(2)}) copy-start(bf16[256,8192]{1,0:T(8,128)(2,1)} %get-tuple-element.148) | copy-start | bytes 12582916 | tf_op jit(solution)/shard_map/while
  98.2 16.2 %copy-start.2 = (s32[32]{0:T(128)S(1)}, s32[32]{0:T(128)}, u32[]{:S(2)}) copy-start(s32[32]{0:T(128)} %param.8) | copy-start | bytes 388
  98.2 16.5 %copy-start.1 = (s32[32,16]{0,1:T(8,128)S(1)}, s32[32,16]{0,1:T(8,128)}, u32[]{:S(2)}) copy-start(s32[32,16]{0,1:T(8,128)} %param.7) | copy-start | bytes 6148
  98.3 16.9 %copy-start.3 = (s32[64]{0:T(128)S(1)}, s32[64]{0:T(128)}, u32[]{:S(2)}) copy-start(s32[64]{0:T(128)} %param.9) | copy-start | bytes 772
  373.4 196.6 %all-to-all-start.1 = ((bf16[128,2,128,2,128]{2,4,1,3,0:T(8,128)(2,1)}), bf16[128,2,128,2,128]{2,4,1,3,0:T(8,128)(2,1)}, u32[]{:S(2)}, u32[]{:S(2)}) async-start(bf16[128,2,128,2,128]{2,4,1,3,0:T(8,128)(2,1)} %copy.34), calls=%async_computation.1 | async-start | bytes 33554432 | tf_op jit(solution)/shard_map/all_to_all | solution.py:127
Sparse Core Ops, SparseCore 0:
  114.6 187.5 all-gather.1
where the time goes:
time: 647 us; the launch traced here: 644 us
  waiting for transfers between devices  368 us (57%)
  local copies, waits for them, and re-layouts  119 us (18%)
  other arithmetic  76.8 us (12%)
  matrix products  35.1 us (5%)
  blocking collectives  15.9 us (2%)
  between operations  13.6 us (2%)
  starting transfers between devices  12.9 us (2%)
    all_gather x1, waiting for transfers between devices, on_device(): incoming = lax.all_gather(quarter, 'chan', axis=0, tiled=True)  186 us
    all_to_all x1, waiting for transfers between devices, on_device(): lax.all_to_all(spectra, 'seg', split_axis=0, concat_axis=4, tiled=True)  181 us
    cos x4, other arithmetic, transform(): table_part = jnp.concatenate([jnp.cos(angles), -jnp.sin(angles)], axis=1)  66.1 us
    reshape x1, local copies, waits for them, and re-layouts, invert(): flat = spectra.reshape(-1, spectra.shape[3] * spectra.shape[4])  27.3 us
    all_to_all x1, local copies, waits for them, and re-layouts, on_device(): lax.all_to_all(spectra, 'seg', split_axis=0, concat_axis=4, tiled=True)  26 us
    another operation x1, local copies, waits for them, and re-layouts, cross_terms(): return jnp.stack([real_part, imag_part], axis=3).astype(jnp.bfloat16)  23.5 us
    all_gather x1, local copies, waits for them, and re-layouts, on_device(): incoming = lax.all_gather(quarter, 'chan', axis=0, tiled=True)  18.6 us
    all_to_all x1, blocking collectives, on_device(): lax.all_to_all(whitened, 'seg', split_axis=3, concat_axis=1, tiled=True)  15.9 us
  transfers between devices with their start and end apart: 2, of which 2 were waited for; matrix products, arithmetic and copies ran while one was open for 1% of the time, Pallas kernels for 0%

commit v1 on v0

--- a/solution.py
+++ b/solution.py
@@ -1,3 +1,4 @@
+import functools
 import math
 import jax
 import jax.numpy as jnp
@@ -10,6 +11,18 @@
 HALF = 8
 LAGS = 256
 TILE_DEV = 2
+
+
+def _fix_yards(page, axis_id, row_dim, dimension_no):
+    return jnp.concatenate(
+        lax.all_to_all(
+            jnp.stack(jnp.split(page, lax.axis_size(axis_id), row_dim), 0), axis_id, 0, 0
+        ),
+        dimension_no,
+    )
+
+
+link_sectors_here = functools.partial(_fix_yards, axis_id="seg", row_dim=3, dimension_no=1)
 
 
 def smoother(bin_count):
@@ -100,7 +113,7 @@
     divisor = jnp.maximum(smoothed, 1.0)
     whitened = jnp.stack([real_part / divisor, imag_part / divisor], axis=1).astype(jnp.bfloat16)
     whitened = whitened.reshape(block_size, local_segs, 2, parts_count, quarter_bins)
-    quarter = lax.all_to_all(whitened, "seg", split_axis=3, concat_axis=1, tiled=True)
+    quarter = link_sectors_here(whitened)
     quarter = quarter.reshape(block_size, all_segs, 2, quarter_bins)
     slot_first, slot_second = pair_blocks(
         pair_offsets, pair_counts, pair_owner, block_count, TILE_DEV * block_count

time: 647 us -> 647 us (level)
  no operation moved by 1% of the time
where the time goes in v1:
time: 647 us; the launch traced here: 644 us
  waiting for transfers between devices  368 us (57%)
  local copies, waits for them, and re-layouts  119 us (18%)
  other arithmetic  76.8 us (12%)
  matrix products  35.1 us (5%)
  blocking collectives  15.9 us (2%)
  between operations  13.6 us (2%)
  starting transfers between devices  12.9 us (2%)
    all_gather x1, waiting for transfers between devices, on_device(): incoming = lax.all_gather(quarter, 'chan', axis=0, tiled=True)  186 us
    all_to_all x1, waiting for transfers between devices, on_device(): lax.all_to_all(spectra, 'seg', split_axis=0, concat_axis=4, tiled=True)  181 us
    cos x4, other arithmetic, transform(): table_part = jnp.concatenate([jnp.cos(angles), -jnp.sin(angles)], axis=1)  66.1 us
    reshape x1, local copies, waits for them, and re-layouts, invert(): flat = spectra.reshape(-1, spectra.shape[3] * spectra.shape[4])  27.3 us
    all_to_all x1, local copies, waits for them, and re-layouts, on_device(): lax.all_to_all(spectra, 'seg', split_axis=0, concat_axis=4, tiled=True)  26 us
    another operation x1, local copies, waits for them, and re-layouts, cross_terms(): return jnp.stack([real_part, imag_part], axis=3).astype(jnp.bfloat16)  23.5 us
    all_gather x1, local copies, waits for them, and re-layouts, on_device(): incoming = lax.all_gather(quarter, 'chan', axis=0, tiled=True)  18.6 us
    all_to_all x1, blocking collectives, _fix_yards(): lax.all_to_all(jnp.stack(jnp.split(page, lax.axis_size(axis_id), row_dim)...  15.9 us
  transfers between devices with their start and end apart: 2, of which 2 were waited for; matrix products, arithmetic and copies ran while one was open for 1% of the time, Pallas kernels for 0%

profile of v1, /device:TPU:1, one launch (start us, length us, event | category | flops | bytes accessed | tf_op | source)
XLA Modules:
  0.0 644.0 jit_solution(6409358491178337120)
XLA Ops:
  6.5 0.1 convert_reduce_fusion
  6.6 7.2 %reshape.214 = bf16[256,8192]{1,0:T(8,128)(2,1)} reshape(bf16[128,2,8192]{2,1,0:T(2,128)(2,1)} %param.6) | data formatting | bytes 8388608 | tf_op jit(solution)/shard_map/reshape | solution.py:83
  13.8 82.4 %while.13 = (s32[]{:T(128)}, f32[4,256,256]{1,2,0:T(8,128)S(1)}, s32[4]{0:T(128)S(1)}, bf16[256,8192]{1,0:T(8,128)(2,1)}, s32[]{:T(128)}, /*index=5*/s32[1]{0:T(128)}, s32[1]{0:T(128)}) while((s32[]{:T(128)}, f32[4,256,256]{1,2,0:T(8,128)S(1)}, s32[4]{0:T(128)S(1)}, bf16[256,8192]{1,0:T(8,128)(2,1)}, s32[]{:T(128)}, ...), condition=%wide.region_8.9_spmd.clone, body=%wide.region_7.8_spmd.clone.sunk | while | flops 2182152192 | bytes 51119252 | solution.py:98
  13.8 0.7 dynamic_slice.19
  15.2 16.5 %fusion.57 = (f32[8192,128]{1,0:T(8,128)S(1)}, f32[8192,128]{1,0:T(8,128)S(1)}) fusion(s32[128]{0:T(128)S(1)} %iota_add_fusion.3), kind=kLoop, calls=%fused_computation.18.clone.1 | loop fusion | flops 15728640 | bytes 8389120 | tf_op jit(solution)/shard_map/while/body/eval_jaxpr/cos | solution.py:92
  31.7 1.3 fusion.58
  33.0 1.3 fusion.59
  34.4 0.7 dynamic_slice.19
  35.7 16.5 %fusion.57 = (f32[8192,128]{1,0:T(8,128)S(1)}, f32[8192,128]{1,0:T(8,128)S(1)}) fusion(s32[128]{0:T(128)S(1)} %iota_add_fusion.3), kind=kLoop, calls=%fused_computation.18.clone.1 | loop fusion | flops 15728640 | bytes 8389120 | tf_op jit(solution)/shard_map/while/body/eval_jaxpr/cos | solution.py:92
  52.3 1.3 fusion.58
  53.6 1.3 fusion.59
  54.9 0.7 dynamic_slice.19
  56.3 16.5 %fusion.57 = (f32[8192,128]{1,0:T(8,128)S(1)}, f32[8192,128]{1,0:T(8,128)S(1)}) fusion(s32[128]{0:T(128)S(1)} %iota_add_fusion.3), kind=kLoop, calls=%fused_computation.18.clone.1 | loop fusion | flops 15728640 | bytes 8389120 | tf_op jit(solution)/shard_map/while/body/eval_jaxpr/cos | solution.py:92
  72.8 1.3 fusion.58
  74.1 1.3 fusion.59
  75.5 0.7 dynamic_slice.19
  76.9 16.5 %fusion.57 = (f32[8192,128]{1,0:T(8,128)S(1)}, f32[8192,128]{1,0:T(8,128)S(1)}) fusion(s32[128]{0:T(128)S(1)} %iota_add_fusion.3), kind=kLoop, calls=%fused_computation.18.clone.1 | loop fusion | flops 15728640 | bytes 8389120 | tf_op jit(solution)/shard_map/while/body/eval_jaxpr/cos | solution.py:92
  93.4 1.3 fusion.58
  94.7 1.3 fusion.59
  96.2 0.4 copy.36
  96.6 0.4 reshape.216
  97.0 1.2 divide_convert_fusion
  98.7 15.9 %all_to_all.20 = bf16[4,128,2,2,1,128]{5,1,4,3,2,0:T(8,128)(2,1)} all-to-all(bf16[4,128,2,2,1,128]{5,1,4,3,2,0:T(8,128)(2,1)S(1)} %pad_maximum_fusion.2), channel_id=1, replica_groups=mesh['chan'=32,'seg'=4] {'seg'}, dimensions={0} | all-to-all | bytes 1048576 | tf_op jit(solution)/shard_map/all_to_all | solution.py:18
  114.6 0.1 copy.34
  114.7 0.1 reduce
  114.9 0.1 convert_reduce_fusion.1
  115.0 0.1 select_reduce_fusion.3
  115.1 0.1 select_reduce_fusion
  115.3 0.1 select_reduce_fusion.2
  115.4 0.1 dynamic_slice.13
  115.7 0.1 fusion.38
  115.8 0.1 compare_and_fusion.1
  115.9 186.4 %all-gather.2.cloned.1.call-done = bf16[4096,8,2,128]{3,0,2,1:T(8,128)(2,1)} async-done(((bf16[128,8,2,128]{3,0,2,1:T(8,128)(2,1)}), bf16[4096,8,2,128]{3,0,2,1:T(8,128)(2,1)}) %all-gather.2.cloned.1.call-update) | async-done | bytes 16777232 | tf_op jit(solution)/shard_map/all_gather | solution.py:129
  302.3 18.6 %copy.41 = bf16[4096,8,2,128]{3,1,2,0:T(8,128)(2,1)} copy(bf16[4096,8,2,128]{3,0,2,1:T(8,128)(2,1)} %all-gather.2.cloned.1.call-done) | data formatting | bytes 33554432 | tf_op jit(solution)/shard_map/all_gather | solution.py:129
  320.8 7.9 %gather_fusion = bf16[4,128,8,2,128]{4,2,3,1,0:T(8,128)(2,1)} fusion(bf16[32,128,8,2,128]{4,2,3,1,0:T(8,128)(2,1)} %bitcast.87, s32[1024]{0:T(1024)S(1)} %pad_clamp_fusion), kind=kCustom, calls=%fused_computation | custom fusion | bytes 4194320 | tf_op jit(solution)/shard_map/jit(_take)/gather | solution.py:133
  328.7 4.2 copy.42
  333.0 0.3 select_select_fusion
  333.3 0.1 fusion.42
  333.4 4.9 fusion.18
  338.3 4.9 fusion.19
  343.2 6.8 %pad_maximum_fusion.1 = bf16[128,2,128,2,128]{0,2,4,1,3:T(8,128)(2,1)} fusion(bf16[128,2,128,1,128]{0,2,4,1,3:T(8,128)(2,1)S(1)} %fusion.19, bf16[128,2,128,1,128]{0,2,4,1,3:T(8,128)(2,1)S(1)} %fusion.18), kind=kLoop, calls=%fused_computation.25 | loop fusion | flops 8388608 | bytes 33554432 | tf_op jit(solution)/shard_map/stack | solution.py:67
  350.0 23.5 %copy.43 = bf16[128,2,128,2,128]{2,4,1,3,0:T(8,128)(2,1)} copy(bf16[128,2,128,2,128]{0,2,4,1,3:T(8,128)(2,1)} %pad_maximum_fusion.1) | data formatting | bytes 33554432 | tf_op jit(solution)/shard_map/stack | solution.py:67
  373.5 12.9 %all-to-all-start.1 = ((bf16[128,2,128,2,128]{2,4,1,3,0:T(8,128)(2,1)}), bf16[128,2,128,2,128]{2,4,1,3,0:T(8,128)(2,1)}, u32[]{:S(2)}, u32[]{:S(2)}) async-start(bf16[128,2,128,2,128]{2,4,1,3,0:T(8,128)(2,1)} %copy.43), calls=%async_computation.1 | async-start | bytes 33554432 | tf_op jit(solution)/shard_map/all_to_all | solution.py:140
  386.4 2.5 cosine_convert_fusion
  388.9 181.2 %all-to-all-done.1 = bf16[128,2,128,2,128]{2,4,1,3,0:T(8,128)(2,1)} async-done(((bf16[128,2,128,2,128]{2,4,1,3,0:T(8,128)(2,1)}), bf16[128,2,128,2,128]{2,4,1,3,0:T(8,128)(2,1)}, u32[]{:S(2)}, u32[]{:S(2)}) %all-to-all-start.1) | async-done | bytes 16777248 | tf_op jit(solution)/shard_map/all_to_all | solution.py:140
  570.1 26.0 %copy.45 = bf16[32,2,128,2,4,128]{5,4,3,2,1,0:T(4,128)(2,1)} copy(bf16[32,2,128,2,4,128]{2,5,1,3,0,4:T(8,128)(2,1)} %bitcast.27) | data formatting | bytes 33554432 | tf_op jit(solution)/shard_map/all_to_all | solution.py:140
  596.1 27.3 %reshape.219 = bf16[8192,1024]{1,0:T(8,128)(2,1)} reshape(bf16[32,2,128,2,4,128]{5,4,3,2,1,0:T(4,128)(2,1)} %copy.45) | data formatting | bytes 33554432 | tf_op jit(solution)/shard_map/reshape | solution.py:71
  623.4 13.7 %convolution_multiply_fusion = f32[8192,256]{1,0:T(8,128)} fusion(bf16[8192,1024]{1,0:T(8,128)(2,1)} %reshape.219, bf16[512,256]{1,0:T(8,128)(2,1)S(1)} %get-tuple-element.103, bf16[512,256]{1,0:T(8,128)(2,1)S(1)} %get-tuple-element.102), kind=kOutput, calls=%fused_computation.28 | convolution fusion | flops 4298113024 | bytes 25690112 | tf_op jit(solution)/shard_map/dot_general | solution.py:72
  (42 shorter events, 0.9 us)
Async XLA Ops:
  6.5 295.7 %all-gather.2.cloned.1.call-start = ((), (), s32[]{:S(2)}) async-start(), calls=%async_computation.2 | async-start | bytes 17301504 | tf_op jit(solution)/shard_map/all_gather | solution.py:129
  15.2 16.5 %copy-start = (bf16[256,8192]{1,0:T(8,128)(2,1)S(1)}, bf16[256,8192]{1,0:T(8,128)(2,1)}, u32[]{:S(2)}) copy-start(bf16[256,8192]{1,0:T(8,128)(2,1)} %get-tuple-element.152) | copy-start | bytes 12582916 | tf_op jit(solution)/shard_map/while
  35.7 16.5 %copy-start = (bf16[256,8192]{1,0:T(8,128)(2,1)S(1)}, bf16[256,8192]{1,0:T(8,128)(2,1)}, u32[]{:S(2)}) copy-start(bf16[256,8192]{1,0:T(8,128)(2,1)} %get-tuple-element.152) | copy-start | bytes 12582916 | tf_op jit(solution)/shard_map/while
  56.3 16.5 %copy-start = (bf16[256,8192]{1,0:T(8,128)(2,1)S(1)}, bf16[256,8192]{1,0:T(8,128)(2,1)}, u32[]{:S(2)}) copy-start(bf16[256,8192]{1,0:T(8,128)(2,1)} %get-tuple-element.152) | copy-start | bytes 12582916 | tf_op jit(solution)/shard_map/while
  76.8 16.5 %copy-start = (bf16[256,8192]{1,0:T(8,128)(2,1)S(1)}, bf16[256,8192]{1,0:T(8,128)(2,1)}, u32[]{:S(2)}) copy-start(bf16[256,8192]{1,0:T(8,128)(2,1)} %get-tuple-element.152) | copy-start | bytes 12582916 | tf_op jit(solution)/shard_map/while
  98.2 16.3 %copy-start.2 = (s32[32]{0:T(128)S(1)}, s32[32]{0:T(128)}, u32[]{:S(2)}) copy-start(s32[32]{0:T(128)} %param.8) | copy-start | bytes 388
  98.2 16.6 %copy-start.1 = (s32[32,16]{0,1:T(8,128)S(1)}, s32[32,16]{0,1:T(8,128)}, u32[]{:S(2)}) copy-start(s32[32,16]{0,1:T(8,128)} %param.7) | copy-start | bytes 6148
  98.3 17.0 %copy-start.3 = (s32[64]{0:T(128)S(1)}, s32[64]{0:T(128)}, u32[]{:S(2)}) copy-start(s32[64]{0:T(128)} %param.9) | copy-start | bytes 772
  373.5 196.6 %all-to-all-start.1 = ((bf16[128,2,128,2,128]{2,4,1,3,0:T(8,128)(2,1)}), bf16[128,2,128,2,128]{2,4,1,3,0:T(8,128)(2,1)}, u32[]{:S(2)}, u32[]{:S(2)}) async-start(bf16[128,2,128,2,128]{2,4,1,3,0:T(8,128)(2,1)} %copy.43), calls=%async_computation.1 | async-start | bytes 33554432 | tf_op jit(solution)/shard_map/all_to_all | solution.py:140
Sparse Core Ops, SparseCore 0:
  114.7 187.5 all-gather.1
